TPU v7x, 256 devices: a whole 4x4x8 slice. The times are simulated.
256 devices in a mesh: rows: 16 (over y, x), feat: 16 (over z, core).
Axes of the slice: x: 4, y: 4, z: 8, core: 2. Of those that a mesh axis runs over, the one named last changes fastest.
Arguments:
- feature_bins: int32 [512, 131072], P('feat', 'rows'), may hold values from 0 to 127
- leaf_index: int32 [131072], P('rows'), may hold values from 0 to 63
- doc_scores: float32 [131072], P('rows'), may hold values from -8 to 256
- doc_weights: float32 [131072], P('rows'), may hold values from 0.3 to 3
- destination: int32 [131072], P('rows'), may hold values from 0 to 131071, as said below
- query_ids: int32 [131072], P('rows'), may hold values from 0 to 131071, as said below
- clicks: int32 [131072], P('rows'), may hold values 0 or 1
Outputs:
- histograms: float32 [64, 512, 2, 128], P('rows', 'feat')
Inputs may be any that keep to these rules, and one draw needn't show every extreme that they name: A permutation of the slots; document i goes to owner destination // 8192, slot destination % 8192; each device's 8192 documents hold exactly 512 for every owner. `query_ids`: a query's id is the number of its last slot; each query's slots are consecutive, lie in one aligned block of 256 slots and hold 1 to 256 slots; every owner's slots hold a query of exactly 256.
All inputs are finite; a program needn't handle non-finite values. No bound on the sum of `clicks` on one device may be relied on, other than what follows from the above.
Results may differ from a plain program's by a relative error of at most 0.0023.
Values may be sent and summed in bfloat16 or wider, within the bound.
No kernel may reach another device: no remote copies, remote signals or barrier semaphores. Data moves between devices by JAX's collectives and lax.ppermute only.
A program may use at most 64 MiB of HBM per device.

v0:
```python
import math
import jax
import jax.numpy as jnp
from jax import lax
from jax.sharding import PartitionSpec as P

BINS = 128
LEAVES = 64
QBLOCK = 256


def block_gradients(approx, weight, query_block, target):
    same_query = query_block[:, None] == query_block[None, :]
    query_top = jnp.max(jnp.where(same_query, approx[None, :], -jnp.inf), axis=1)
    scaled = weight * jnp.exp(approx - query_top)
    matrix = same_query.astype(jnp.float32)
    denominator = jnp.dot(matrix, scaled, precision=lax.Precision.HIGHEST)
    clicked = jnp.dot(matrix, weight * target, precision=lax.Precision.HIGHEST)
    chance = scaled / denominator
    gradient = (weight * target - clicked * chance).astype(jnp.bfloat16)
    curvature = (clicked * chance * (1.0 - chance)).astype(jnp.bfloat16)
    return (gradient, curvature)


def query_gradients(approx, weight, query_ids, clicks):
    doc_count = approx.shape[0]
    nblocks = doc_count // QBLOCK
    per_step = 2
    shaped = lambda arr: arr.reshape(nblocks // per_step, per_step, QBLOCK)
    target = clicks.astype(jnp.float32)

    def step_blocks(inputs):
        return jax.vmap(block_gradients)(*inputs)

    gradient, curvature = lax.map(
        step_blocks, (shaped(approx), shaped(weight), shaped(query_ids), shaped(target))
    )
    return jnp.stack([gradient.reshape(doc_count), curvature.reshape(doc_count)])


def shards(feature_bins, leaf_index, doc_scores, doc_weights, destination, query_ids, clicks):
    owners = lax.axis_size("rows")
    doc_count = destination.shape[0]
    capacity = doc_count // owners
    ranking = jnp.argsort(destination)
    sorted_dest = destination[ranking]
    values = jnp.stack([doc_scores[ranking], doc_weights[ranking]]).reshape(2, owners, capacity)
    slot_ids = (sorted_dest % doc_count).reshape(owners, capacity)
    arrived = lax.all_to_all(values, "rows", split_axis=1, concat_axis=1, tiled=True)
    slot_in = lax.all_to_all(slot_ids, "rows", split_axis=0, concat_axis=0, tiled=True)
    owner_values = (
        jnp.zeros((2, doc_count), jnp.float32)
        .at[:, slot_in.reshape(-1)]
        .set(arrived.reshape(2, doc_count))
    )
    owner_stats = query_gradients(owner_values[0], owner_values[1], query_ids, clicks)
    outgoing = owner_stats[:, slot_in]
    returned = lax.all_to_all(outgoing, "rows", split_axis=1, concat_axis=1, tiled=True)
    doc_stats = (
        jnp.zeros((2, doc_count), jnp.bfloat16).at[:, ranking].set(returned.reshape(2, doc_count))
    )
    stats_rows = doc_stats.T
    f_dev = feature_bins.shape[0]
    bunch_size = math.gcd(4, f_dev)
    columns = feature_bins.reshape(f_dev // bunch_size, bunch_size, doc_count)
    bin_range = jnp.arange(BINS, dtype=jnp.int32)
    share = LEAVES // owners
    leaf_hot = (leaf_index[:, None] == jnp.arange(LEAVES, dtype=jnp.int32)[None, :]).astype(
        jnp.bfloat16
    )
    spread = (leaf_hot[:, :, None] * stats_rows[:, None, :]).reshape(doc_count, LEAVES * 2)

    def per_bunch(bunch):
        one_hot = (bunch[:, :, None] == bin_range).astype(jnp.bfloat16)
        return jnp.einsum("gdb,dk->gkb", one_hot, spread, preferred_element_type=jnp.float32)

    pieces = lax.map(per_bunch, columns).reshape(f_dev, LEAVES, 2, BINS)
    summed = lax.psum(jnp.transpose(pieces, (1, 0, 2, 3)), "rows")
    return lax.dynamic_slice_in_dim(summed, lax.axis_index("rows") * share, share, 0)


def solution(mesh):
    placed = (P("feat", "rows"), P("rows"), P("rows"), P("rows"), P("rows"), P("rows"), P("rows"))
    return jax.shard_map(
        shards, mesh=mesh, in_specs=placed, out_specs=P("rows", "feat", None, None), check_vma=False
    )
```

profile of v0, /device:TPU:2, one launch (start us, length us, event | category | flops | bytes accessed | tf_op | source)
XLA Modules:
  0.0 488.9 jit_solution(7182979089565845534)
XLA Ops:
  6.5 7.6 %sort.17 = (s32[8192]{0:T(1024)}, s32[8192]{0:T(1024)S(1)}) sort(s32[8192]{0:T(1024)} %param.15, s32[8192]{0:T(1024)S(1)} %iota.15), dimensions={0}, to_apply=%region_0.0 | sort | flops 106496 | bytes 131072 | tf_op jit(solution)/shard_map/jit(argsort)/sort | solution.py:45
  14.2 45.5 %gather_fusion = s32[8192]{0:T(1024)S(1)} fusion(s32[8192]{0:T(1024)S(1)} %copy-done.1, s32[8192]{0:T(1024)S(1)} %get-tuple-element.140), kind=kCustom, calls=%fused_computation | custom fusion | bytes 98304 | tf_op jit(solution)/shard_map/gather | solution.py:46
  60.4 7.5 %all-to-all-start = ((s32[16,1,512]{2,1,0:T(1,128)}), s32[16,1,512]{2,1,0:T(1,128)S(1)}, u32[]{:S(2)}, u32[]{:S(2)}) async-start(s32[16,1,512]{2,1,0:T(1,128)} %and_select_fusion), calls=%async_computation | async-start | bytes 65536 | tf_op jit(solution)/shard_map/all_to_all | solution.py:50
  67.9 45.5 %gather_fusion.1 = f32[8192]{0:T(1024)S(1)} fusion(f32[8192]{0:T(1024)S(1)} %copy-done, s32[8192]{0:T(1024)S(1)} %get-tuple-element.140), kind=kCustom, calls=%fused_computation.1 | custom fusion | bytes 98304 | tf_op jit(solution)/shard_map/gather | solution.py:47
  114.2 45.5 %gather_fusion.2 = f32[8192]{0:T(1024)S(1)} fusion(f32[8192]{0:T(1024)S(1)} %copy-done.2, s32[8192]{0:T(1024)S(1)} %get-tuple-element.140), kind=kCustom, calls=%fused_computation.2 | custom fusion | bytes 98304 | tf_op jit(solution)/shard_map/gather | solution.py:47
  160.5 7.2 %all-to-all-start.1 = ((f32[2,16,512]{2,0,1:T(2,128)}), f32[2,16,512]{2,0,1:T(2,128)S(1)}, u32[]{:S(2)}, u32[]{:S(2)}) async-start(f32[2,16,512]{2,0,1:T(2,128)} %copy.32), calls=%async_computation.1 | async-start | bytes 131072 | tf_op jit(solution)/shard_map/all_to_all | solution.py:49
  167.9 6.2 %all-to-all-done.1 = f32[2,16,512]{2,0,1:T(2,128)S(1)} async-done(((f32[2,16,512]{2,0,1:T(2,128)}), f32[2,16,512]{2,0,1:T(2,128)S(1)}, u32[]{:S(2)}, u32[]{:S(2)}) %all-to-all-start.1) | async-done | bytes 65568 | tf_op jit(solution)/shard_map/all_to_all | solution.py:49
  174.1 2.6 copy.33
  176.7 23.0 %scatter_custom_fusion = f32[2,8192]{0,1:T(8,128)} fusion(s32[8192]{0:T(1024)S(1)} %bitcast.107, f32[8192,2]{1,0:T(8,128)} %copy.33, f32[]{:T(128)} %constant.54.clone.1), kind=kCustom, calls=%fused_computation.44 | custom fusion | bytes 66048 | tf_op jit(solution)/shard_map/scatter | solution.py:54
  199.7 6.8 %slice_reduce_fusion = (f32[8192]{0:T(1024)S(1)}, f32[8192]{0:T(1024)S(1)}) fusion(f32[2,8192]{0,1:T(8,128)} %scatter_custom_fusion), kind=kLoop, calls=%fused_computation.42 | loop fusion | bytes 131072 | tf_op jit(solution)/shard_map/slice | solution.py:56
  206.5 18.5 %while.23 = (s32[]{:T(128)}, bf16[16,2,256]{2,1,0:T(2,128)(2,1)S(1)}, bf16[16,2,256]{2,1,0:T(2,128)(2,1)S(1)}, f32[16,2,256]{2,1,0:T(2,128)S(1)}, f32[16,2,256]{...) while((s32[]{:T(128)}, bf16[16,2,256]{2,1,0:T(2,128)(2,1)S(1)}, ...), condition=%wide.region_4.5_spmd, body=%wide.region_2.4_spmd.sunk | while | flops 3806722 | bytes 57449 | solution.py:35
  225.2 1.1 copy.34
  226.3 29.2 %gather_fusion.3 = bf16[8192,2]{1,0:T(8,128)(2,1)} fusion(bf16[2,8192]{0,1:T(8,128)(2,1)S(1)} %copy.34, s32[8192]{0:T(1024)S(1)} %broadcast_clamp_fusion), kind=kCustom, calls=%fused_computation.3 | custom fusion | bytes 98304 | tf_op jit(solution)/shard_map/gather | solution.py:57
  255.6 2.6 copy.35
  258.2 4.7 all-to-all-start.2
  263.2 1.3 reshape.175
  264.4 4.8 all-to-all-done.2
  269.2 1.8 copy.36
  271.0 22.1 %scatter_custom_fusion.1 = bf16[2,8192]{0,1:T(8,128)(2,1)S(1)} fusion(s32[8192]{0:T(1024)S(1)} %get-tuple-element.141, bf16[8192,2]{1,0:T(8,128)(2,1)} %copy.36, bf16[]{:T(256)} %constant.55.clone.1), kind=kCustom, calls=%fused_computation.48 | custom fusion | bytes 33280 | tf_op jit(solution)/shard_map/scatter | solution.py:60
  294.1 85.1 %while.24 = (s32[]{:T(128)}, f32[8,4,128,128]{3,2,1,0:T(8,128)}, s32[8,4,8192]{2,1,0:T(4,128)}, bf16[8192,2]{0,1:T(2,128)(2,1)S(1)}, bf16[8192,64]{0,1:T(8,128)(2,1)S(1)}, /*index=5*/s32[]{:T(128)}) while((s32[]{:T(128)}, f32[8,4,128,128]{3,2,1,0:T(8,128)}, s32[8,4,8192]{2,1,0:T(4,128)}, bf16[8192,2]{0,1:T(2,128)(2,1)S(1)}, ...), condition=%wide.region_7.8_spmd.clone, body=%wide.region_6.7_spmd.clone.sunk | while | flops 1078984704 | bytes 11174473 | solution.py:77
  294.1 0.9 dynamic-slice_bitcast_fusion.8
  295.0 2.2 broadcast_multiply_fusion.2
  297.2 2.2 mul.91
  299.5 4.4 fusion.47
  305.6 2.2 broadcast_multiply_fusion.2
  307.9 2.2 mul.91
  310.1 4.4 fusion.47
  316.3 2.2 broadcast_multiply_fusion.2
  318.5 2.2 mul.91
  320.7 4.4 fusion.47
  326.0 0.9 dynamic-slice_bitcast_fusion.8
  326.9 2.2 broadcast_multiply_fusion.2
  329.1 2.2 mul.91
  331.4 4.4 fusion.47
  337.5 2.2 broadcast_multiply_fusion.2
  339.8 2.2 mul.91
  342.0 4.4 fusion.47
  348.2 2.2 broadcast_multiply_fusion.2
  350.4 2.2 mul.91
  352.6 4.4 fusion.47
  358.8 2.2 broadcast_multiply_fusion.2
  361.1 2.2 mul.91
  363.3 4.4 fusion.47
  369.5 2.2 broadcast_multiply_fusion.2
  371.7 2.2 mul.91
  373.9 4.4 fusion.47
  379.2 101.2 %all-reduce.2.cloned.1.call-done = f32[64,32,2,128]{3,2,0,1:T(2,128)} async-done(((f32[64,32,2,128]{3,2,0,1:T(2,128)}), f32[64,32,2,128]{3,2,0,1:T(2,128)}) %all-reduce.2.cloned.1.call-update) | async-done | bytes 2097168 | tf_op jit(solution)/shard_map/psum | solution.py:78
  480.4 0.9 constant_dynamic-slice_fusion.1
  (191 shorter events, 34.5 us)
Async XLA Ops:
  6.5 61.3 %copy-start = (f32[8192]{0:T(1024)S(1)}, f32[8192]{0:T(1024)}, u32[]{:S(2)}) copy-start(f32[8192]{0:T(1024)} %param.13) | copy-start | bytes 98308
  6.5 7.6 %copy-start.1 = (s32[8192]{0:T(1024)S(1)}, s32[8192]{0:T(1024)}, u32[]{:S(2)}) copy-start(s32[8192]{0:T(1024)} %param.15) | copy-start | bytes 98308
  60.4 100.1 %all-to-all-start = ((s32[16,1,512]{2,1,0:T(1,128)}), s32[16,1,512]{2,1,0:T(1,128)S(1)}, u32[]{:S(2)}, u32[]{:S(2)}) async-start(s32[16,1,512]{2,1,0:T(1,128)} %and_select_fusion), calls=%async_computation | async-start | bytes 65536 | tf_op jit(solution)/shard_map/all_to_all | solution.py:50
  113.4 0.8 copy-start.2
  114.2 46.3 %copy-start.5 = (s32[8192]{0:T(1024)S(1)}, s32[8192]{0:T(1024)}, u32[]{:S(2)}) copy-start(s32[8192]{0:T(1024)} %param.17) | copy-start | bytes 98308
  114.2 46.3 %copy-start.6 = (s32[8192]{0:T(1024)S(1)}, s32[8192]{0:T(1024)}, u32[]{:S(2)}) copy-start(s32[8192]{0:T(1024)} %param.16) | copy-start | bytes 98308
  160.5 13.5 %all-to-all-start.1 = ((f32[2,16,512]{2,0,1:T(2,128)}), f32[2,16,512]{2,0,1:T(2,128)S(1)}, u32[]{:S(2)}, u32[]{:S(2)}) async-start(f32[2,16,512]{2,0,1:T(2,128)} %copy.32), calls=%async_computation.1 | async-start | bytes 131072 | tf_op jit(solution)/shard_map/all_to_all | solution.py:49
  225.2 37.7 %copy-start.4 = (s32[8192]{0:T(1024)S(1)}, s32[8192]{0:T(1024)}, u32[]{:S(2)}) copy-start(s32[8192]{0:T(1024)} %param.12) | copy-start | bytes 98308
  226.3 36.9 %copy-start.3 = (s32[32,8192]{1,0:T(8,128)S(1)}, s32[32,8192]{1,0:T(8,128)}, u32[]{:S(2)}) copy-start(s32[32,8192]{1,0:T(8,128)} %param.11) | copy-start | bytes 3145732
  258.2 11.0 %all-to-all-start.2 = ((bf16[2,16,512]{2,0,1:T(2,128)(2,1)}), bf16[2,16,512]{2,0,1:T(2,128)(2,1)S(1)}, u32[]{:S(2)}, u32[]{:S(2)}) async-start(bf16[2,16,512]{2,0,1:T(2,128)(2,1)} %bitcast.18), calls=%async_computation.2 | async-start | bytes 65536 | tf_op jit(solution)/shard_map/all_to_all | solution.py:58
  262.9 217.5 %all-reduce.2.cloned.1.call-start = ((), (), s32[]{:S(2)}) async-start(), calls=%async_computation.3 | async-start | bytes 4194304 | tf_op jit(solution)/shard_map/psum | solution.py:78
Sparse Core Ops, SparseCore 0:
  379.3 101.0 all-reduce.1
where the time goes:
time: 490 us; the launch traced here: 489 us
  local copies, waits for them, and re-layouts  264 us (54%)
  waiting for transfers between devices  112 us (23%)
  matrix products  47.3 us (10%)
  other arithmetic  31.6 us (6%)
  starting transfers between devices  19.5 us (4%)
  between operations  13.7 us (3%)
    psum x1, waiting for transfers between devices, shards(): summed = lax.psum(jnp.transpose(pieces, (1, 0, 2, 3)), 'rows')  101 us
    gather x1, local copies, waits for them, and re-layouts, shards(): sorted_dest = destination[ranking]  45.5 us
    gather x1, local copies, waits for them, and re-layouts, shards(): doc_scores[ranking]  45.5 us
    gather x1, local copies, waits for them, and re-layouts, shards(): doc_weights[ranking]  45.5 us
    dot_general x8, matrix products, per_bunch(): jnp.einsum('gdb,dk->gkb', one_hot, spread, preferred_element_type=jnp.flo...  35 us
    gather x2, local copies, waits for them, and re-layouts, shards(): outgoing = owner_stats[:, slot_in]  31.8 us
    scatter x1, local copies, waits for them, and re-layouts, shards(): owner_values = jnp.zeros((2, doc_count), jnp.float32).at[:, slot_in.resha...  23 us
    scatter x1, local copies, waits for them, and re-layouts, shards(): jnp.zeros((2, doc_count), jnp.bfloat16).at[:, ranking]  22.1 us
  transfers between devices with their start and end apart: 4, of which 3 were waited for; matrix products, arithmetic and copies ran while one was open for 19% of the time, Pallas kernels for 0%

commit v1 on v0

--- a/solution.py
+++ b/solution.py
@@ -75,7 +75,7 @@
         return jnp.einsum("gdb,dk->gkb", one_hot, spread, preferred_element_type=jnp.float32)
 
     pieces = lax.map(per_bunch, columns).reshape(f_dev, LEAVES, 2, BINS)
-    summed = lax.psum(jnp.transpose(pieces, (1, 0, 2, 3)), "rows")
+    summed = jnp.sum(lax.all_gather(jnp.transpose(pieces, (1, 0, 2, 3)), "rows"), axis=0)
     return lax.dynamic_slice_in_dim(summed, lax.axis_index("rows") * share, share, 0)
 
 

time: 490 us -> 603 us (1.23)
  waiting for transfers between devices: 112 us -> 213 us
  other arithmetic: 31.6 us -> 44.4 us
    all_gather x0 -> x1, waiting for transfers between devices: none -> 202 us  [shards(): lax.all_gather(jnp.transpose(pieces, (1, 0, 2, 3)), 'rows')]
    psum x1 -> x0, waiting for transfers between devices: 101 us -> none  [shards(): summed = lax.psum(jnp.transpose(pieces, (1, 0, 2, 3)), 'rows')]
    reduce_sum x0 -> x1, other arithmetic: none -> 12.8 us  [shards(): jnp.sum(lax.all_gather(jnp.transpose(pieces, (1, 0, 2, 3)), 'rows'), axis=0)]
  transfers between devices with their start and end apart: 4 -> 4, of which waited for: 3 -> 3; matrix products, arithmetic and copies ran while one was open for 19% -> 16% of each run, Pallas kernels for 0% -> 0%
where the time goes in v1:
time: 603 us; the launch traced here: 602 us
  local copies, waits for them, and re-layouts  263 us (44%)
  waiting for transfers between devices  213 us (35%)
  matrix products  47.3 us (8%)
  other arithmetic  44.4 us (7%)
  starting transfers between devices  19.5 us (3%)
  between operations  13.7 us (2%)
    all_gather x1, waiting for transfers between devices, shards(): lax.all_gather(jnp.transpose(pieces, (1, 0, 2, 3)), 'rows')  202 us
    gather x1, local copies, waits for them, and re-layouts, shards(): sorted_dest = destination[ranking]  45.5 us
    gather x1, local copies, waits for them, and re-layouts, shards(): doc_scores[ranking]  45.5 us
    gather x1, local copies, waits for them, and re-layouts, shards(): doc_weights[ranking]  45.5 us
    dot_general x8, matrix products, per_bunch(): jnp.einsum('gdb,dk->gkb', one_hot, spread, preferred_element_type=jnp.flo...  35 us
    gather x2, local copies, waits for them, and re-layouts, shards(): outgoing = owner_stats[:, slot_in]  31.8 us
    scatter x1, local copies, waits for them, and re-layouts, shards(): owner_values = jnp.zeros((2, doc_count), jnp.float32).at[:, slot_in.resha...  23 us
    scatter x1, local copies, waits for them, and re-layouts, shards(): jnp.zeros((2, doc_count), jnp.bfloat16).at[:, ranking]  22.1 us
  transfers between devices with their start and end apart: 4, of which 3 were waited for; matrix products, arithmetic and copies ran while one was open for 16% of the time, Pallas kernels for 0%

profile of v1, /device:TPU:2, one launch (start us, length us, event | category | flops | bytes accessed | tf_op | source)
XLA Modules:
  0.0 601.9 jit_solution(1001898832791064327)
XLA Ops:
  6.5 7.6 %sort.17 = (s32[8192]{0:T(1024)}, s32[8192]{0:T(1024)S(1)}) sort(s32[8192]{0:T(1024)} %param.15, s32[8192]{0:T(1024)S(1)} %iota.15), dimensions={0}, to_apply=%region_0.0 | sort | flops 106496 | bytes 131072 | tf_op jit(solution)/shard_map/jit(argsort)/sort | solution.py:45
  14.2 45.5 %gather_fusion = s32[8192]{0:T(1024)S(1)} fusion(s32[8192]{0:T(1024)S(1)} %copy-done.1, s32[8192]{0:T(1024)S(1)} %get-tuple-element.140), kind=kCustom, calls=%fused_computation | custom fusion | bytes 98304 | tf_op jit(solution)/shard_map/gather | solution.py:46
  60.4 7.5 %all-to-all-start = ((s32[16,1,512]{2,1,0:T(1,128)}), s32[16,1,512]{2,1,0:T(1,128)S(1)}, u32[]{:S(2)}, u32[]{:S(2)}) async-start(s32[16,1,512]{2,1,0:T(1,128)} %and_select_fusion), calls=%async_computation | async-start | bytes 65536 | tf_op jit(solution)/shard_map/all_to_all | solution.py:50
  67.9 45.5 %gather_fusion.1 = f32[8192]{0:T(1024)S(1)} fusion(f32[8192]{0:T(1024)S(1)} %copy-done, s32[8192]{0:T(1024)S(1)} %get-tuple-element.140), kind=kCustom, calls=%fused_computation.1 | custom fusion | bytes 98304 | tf_op jit(solution)/shard_map/gather | solution.py:47
  114.2 45.5 %gather_fusion.2 = f32[8192]{0:T(1024)S(1)} fusion(f32[8192]{0:T(1024)S(1)} %copy-done.2, s32[8192]{0:T(1024)S(1)} %get-tuple-element.140), kind=kCustom, calls=%fused_computation.2 | custom fusion | bytes 98304 | tf_op jit(solution)/shard_map/gather | solution.py:47
  160.5 7.2 %all-to-all-start.1 = ((f32[2,16,512]{2,0,1:T(2,128)}), f32[2,16,512]{2,0,1:T(2,128)S(1)}, u32[]{:S(2)}, u32[]{:S(2)}) async-start(f32[2,16,512]{2,0,1:T(2,128)} %copy.31), calls=%async_computation.1 | async-start | bytes 131072 | tf_op jit(solution)/shard_map/all_to_all | solution.py:49
  167.9 6.2 %all-to-all-done.1 = f32[2,16,512]{2,0,1:T(2,128)S(1)} async-done(((f32[2,16,512]{2,0,1:T(2,128)}), f32[2,16,512]{2,0,1:T(2,128)S(1)}, u32[]{:S(2)}, u32[]{:S(2)}) %all-to-all-start.1) | async-done | bytes 65568 | tf_op jit(solution)/shard_map/all_to_all | solution.py:49
  174.1 2.6 copy.32
  176.7 23.0 %scatter_custom_fusion = f32[2,8192]{0,1:T(8,128)} fusion(s32[8192]{0:T(1024)S(1)} %bitcast.109, f32[8192,2]{1,0:T(8,128)} %copy.32, f32[]{:T(128)} %constant.40.clone.1), kind=kCustom, calls=%fused_computation.44 | custom fusion | bytes 66048 | tf_op jit(solution)/shard_map/scatter | solution.py:54
  199.7 6.8 %slice_reduce_fusion = (f32[8192]{0:T(1024)S(1)}, f32[8192]{0:T(1024)S(1)}) fusion(f32[2,8192]{0,1:T(8,128)} %scatter_custom_fusion), kind=kLoop, calls=%fused_computation.42 | loop fusion | bytes 131072 | tf_op jit(solution)/shard_map/slice | solution.py:56
  206.5 18.5 %while.23 = (s32[]{:T(128)}, bf16[16,2,256]{2,1,0:T(2,128)(2,1)S(1)}, bf16[16,2,256]{2,1,0:T(2,128)(2,1)S(1)}, f32[16,2,256]{2,1,0:T(2,128)S(1)}, f32[16,2,256]{...) while((s32[]{:T(128)}, bf16[16,2,256]{2,1,0:T(2,128)(2,1)S(1)}, ...), condition=%wide.region_4.5_spmd, body=%wide.region_2.4_spmd.sunk | while | flops 3806722 | bytes 57449 | solution.py:35
  225.2 1.1 copy.33
  226.3 29.2 %gather_fusion.3 = bf16[8192,2]{1,0:T(8,128)(2,1)} fusion(bf16[2,8192]{0,1:T(8,128)(2,1)S(1)} %copy.33, s32[8192]{0:T(1024)S(1)} %broadcast_clamp_fusion), kind=kCustom, calls=%fused_computation.3 | custom fusion | bytes 98304 | tf_op jit(solution)/shard_map/gather | solution.py:57
  255.6 2.6 copy.34
  258.2 4.7 all-to-all-start.2
  263.2 1.3 reshape.175
  264.5 4.7 all-to-all-done.2
  269.2 1.9 copy.35
  271.1 22.1 %scatter_custom_fusion.1 = bf16[2,8192]{0,1:T(8,128)(2,1)S(1)} fusion(s32[8192]{0:T(1024)S(1)} %get-tuple-element.141, bf16[8192,2]{1,0:T(8,128)(2,1)} %copy.35, bf16[]{:T(256)} %constant.56.clone.1), kind=kCustom, calls=%fused_computation.48 | custom fusion | bytes 33280 | tf_op jit(solution)/shard_map/scatter | solution.py:60
  294.1 85.1 %while.24 = (s32[]{:T(128)}, f32[8,4,128,128]{3,2,1,0:T(8,128)}, s32[8,4,8192]{2,1,0:T(4,128)}, bf16[8192,2]{0,1:T(2,128)(2,1)S(1)}, bf16[8192,64]{0,1:T(8,128)(2,1)S(1)}, /*index=5*/s32[]{:T(128)}) while((s32[]{:T(128)}, f32[8,4,128,128]{3,2,1,0:T(8,128)}, s32[8,4,8192]{2,1,0:T(4,128)}, bf16[8192,2]{0,1:T(2,128)(2,1)S(1)}, ...), condition=%wide.region_7.8_spmd.clone, body=%wide.region_6.7_spmd.clone.sunk | while | flops 1078984704 | bytes 11174473 | solution.py:77
  294.2 0.9 dynamic-slice_bitcast_fusion.8
  295.1 2.2 broadcast_multiply_fusion.2
  297.3 2.2 mul.91
  299.5 4.4 fusion.47
  305.7 2.2 broadcast_multiply_fusion.2
  307.9 2.2 mul.91
  310.2 4.4 fusion.47
  315.4 0.9 dynamic-slice_bitcast_fusion.8
  316.3 2.2 broadcast_multiply_fusion.2
  318.5 2.2 mul.91
  320.8 4.4 fusion.47
  326.9 2.2 broadcast_multiply_fusion.2
  329.2 2.2 mul.91
  331.4 4.4 fusion.47
  337.6 2.2 broadcast_multiply_fusion.2
  339.8 2.2 mul.91
  342.1 4.4 fusion.47
  348.2 2.2 broadcast_multiply_fusion.2
  350.4 2.2 mul.91
  352.7 4.4 fusion.47
  358.9 2.2 broadcast_multiply_fusion.2
  361.1 2.2 mul.91
  363.3 4.4 fusion.47
  369.5 2.2 broadcast_multiply_fusion.2
  371.7 2.2 mul.91
  373.9 4.4 fusion.47
  379.2 202.3 %all-gather.3.cloned.1.call-done = f32[1024,32,2,128]{3,2,0,1:T(2,128)} async-done(((f32[64,32,2,128]{3,2,0,1:T(2,128)}), f32[1024,32,2,128]{3,2,0,1:T(2,128)}) %all-gather.3.cloned.1.call-update) | async-done | bytes 33554448 | tf_op jit(solution)/shard_map/all_gather | solution.py:78
  581.5 12.8 %reduce_sum.9 = f32[64,32,2,128]{3,2,0,1:T(2,128)S(1)} reduce(f32[16,64,32,2,128]{4,3,1,0,2:T(2,128)} %bitcast.99, f32[]{:T(128)} %constant.40.clone.1), dimensions={0}, to_apply=%region_8.9 | reduce | flops 7864320 | bytes 35651588 | tf_op jit(solution)/shard_map/reduce_sum | solution.py:78
  (192 shorter events, 34.5 us)
Async XLA Ops:
  6.5 61.3 %copy-start = (f32[8192]{0:T(1024)S(1)}, f32[8192]{0:T(1024)}, u32[]{:S(2)}) copy-start(f32[8192]{0:T(1024)} %param.13) | copy-start | bytes 98308
  6.5 7.6 %copy-start.1 = (s32[8192]{0:T(1024)S(1)}, s32[8192]{0:T(1024)}, u32[]{:S(2)}) copy-start(s32[8192]{0:T(1024)} %param.15) | copy-start | bytes 98308
  60.4 100.1 %all-to-all-start = ((s32[16,1,512]{2,1,0:T(1,128)}), s32[16,1,512]{2,1,0:T(1,128)S(1)}, u32[]{:S(2)}, u32[]{:S(2)}) async-start(s32[16,1,512]{2,1,0:T(1,128)} %and_select_fusion), calls=%async_computation | async-start | bytes 65536 | tf_op jit(solution)/shard_map/all_to_all | solution.py:50
  113.4 0.8 copy-start.2
  114.2 46.3 %copy-start.5 = (s32[8192]{0:T(1024)S(1)}, s32[8192]{0:T(1024)}, u32[]{:S(2)}) copy-start(s32[8192]{0:T(1024)} %param.17) | copy-start | bytes 98308
  114.2 46.3 %copy-start.6 = (s32[8192]{0:T(1024)S(1)}, s32[8192]{0:T(1024)}, u32[]{:S(2)}) copy-start(s32[8192]{0:T(1024)} %param.16) | copy-start | bytes 98308
  160.5 13.5 %all-to-all-start.1 = ((f32[2,16,512]{2,0,1:T(2,128)}), f32[2,16,512]{2,0,1:T(2,128)S(1)}, u32[]{:S(2)}, u32[]{:S(2)}) async-start(f32[2,16,512]{2,0,1:T(2,128)} %copy.31), calls=%async_computation.1 | async-start | bytes 131072 | tf_op jit(solution)/shard_map/all_to_all | solution.py:49
  225.2 37.7 %copy-start.4 = (s32[8192]{0:T(1024)S(1)}, s32[8192]{0:T(1024)}, u32[]{:S(2)}) copy-start(s32[8192]{0:T(1024)} %param.12) | copy-start | bytes 98308
  226.3 36.9 %copy-start.3 = (s32[32,8192]{1,0:T(8,128)S(1)}, s32[32,8192]{1,0:T(8,128)}, u32[]{:S(2)}) copy-start(s32[32,8192]{1,0:T(8,128)} %param.11) | copy-start | bytes 3145732
  258.2 11.0 %all-to-all-start.2 = ((bf16[2,16,512]{2,0,1:T(2,128)(2,1)}), bf16[2,16,512]{2,0,1:T(2,128)(2,1)S(1)}, u32[]{:S(2)}, u32[]{:S(2)}) async-start(bf16[2,16,512]{2,0,1:T(2,128)(2,1)} %bitcast.18), calls=%async_computation.2 | async-start | bytes 65536 | tf_op jit(solution)/shard_map/all_to_all | solution.py:58
  262.9 318.6 %all-gather.3.cloned.1.call-start = ((), (), s32[]{:S(2)}) async-start(), calls=%async_computation.3 | async-start | bytes 35651584 | tf_op jit(solution)/shard_map/all_gather | solution.py:78
Sparse Core Ops, SparseCore 0:
  379.3 202.1 all-gather.2
